TPU v7x, 256 devices: a whole 4x4x8 slice. The times are simulated.
256 devices in a mesh: blk: 64 (over y_lo, z, x), rep: 4 (over y_hi, core).
Axes of the slice: x: 4, y: 4 (y_hi: 2, y_lo: 2; y = y_hi * 2 + y_lo), z: 8, core: 2. Of those that a mesh axis runs over, the one named last changes fastest.
Arguments:
- features: bfloat16 [262144, 128], P(('blk', 'rep')), may hold values from -6 to 6
- weight: bfloat16 [128, 512], replicated, may hold values from -0.5 to 0.5
- bias: float32 [512], replicated, may hold values from -3 to 3
- tile_values: bfloat16 [262144, 4096], P(('blk', 'rep')), may hold values from -0.125 to 0.125
- tile_cols: int32 [2048, 32], P(('blk', 'rep')), may hold values from 0 to 95, as said below
- tile_counts: int32 [2048], P(('blk', 'rep')), may hold values from 1 to 32, as said below
- out_grad: bfloat16 [262144, 512], P(('blk', 'rep')), may hold values from -6 to 6
Outputs:
- activations: bfloat16 [262144, 512], P(('blk', 'rep'))
- feature_grad: float32 [262144, 128], P(('blk', 'rep'))
- weight_grad: float32 [128, 512], replicated
- bias_grad: float32 [512], replicated
Inputs may be any that keep to these rules, and one draw needn't show every extreme that they name: `tile_cols`: within one row tile the 32 entries are different. `tile_counts`: slots 0 to count - 1 of a row tile are live.
All inputs are finite; a program needn't handle non-finite values.
Results may differ from a plain program's by a relative error of at most 0.0059.
Values may be sent and summed in bfloat16 or wider, within the bound.
No kernel may reach another device: no remote copies, remote signals or barrier semaphores. Data moves between devices by JAX's collectives and lax.ppermute only.
A program may use at most 128 MiB of HBM per device.

v0:
```python
import math
import jax
import jax.numpy as jnp
from jax import lax
from jax.sharding import PartitionSpec as P

TILE = 128
REACH = 1
SLOTS = 32


def passed_along(value, axis, steps):
    count = lax.axis_size(axis)
    pairs = [(source, (source + steps) % count) for source in range(count)]
    return lax.ppermute(value, axis, pairs)


def in_blocks(shard, dim, length):
    before, after = (shard.shape[:dim], shard.shape[dim + 1 :])
    return jnp.moveaxis(shard.reshape(*before, length, -1, *after), dim, 0)


def summed_on_arrival(shard, axis, dim):
    length = lax.axis_size(axis)
    pieces = lax.all_to_all(in_blocks(shard, dim, length), axis, 0, 0, tiled=True)
    return jnp.sum(pieces, axis=0)


def gelu_parts(pre_act):
    inner = 0.7978845608028654 * (pre_act + 0.044715 * pre_act * pre_act * pre_act)
    tangent = jnp.tanh(inner)
    value_part = 0.5 * pre_act * (1.0 + tangent)
    slope = 0.5 * (1.0 + tangent) + 0.5 * pre_act * (
        1.0 - tangent * tangent
    ) * 0.7978845608028654 * (1.0 + 0.134145 * pre_act * pre_act)
    return (value_part, slope)


def on_device(features, weight, bias, tile_values, tile_cols, tile_counts, out_grad):
    rows_dev, in_dim = features.shape
    row_tiles = rows_dev // TILE
    group_size = lax.axis_size("rep")
    block_rows = rows_dev * group_size
    nodes = block_rows * lax.axis_size("blk")
    offsets = list(range(-REACH, REACH + 1))
    pieces = []
    for offset_now in offsets:
        if offset_now == 0:
            pieces.append(features)
        else:
            pieces.append(passed_along(features, "blk", -offset_now))
    stacked = jnp.stack(pieces)
    window = lax.all_gather(stacked, "rep", axis=1, tiled=True).reshape(-1, in_dim)
    window_tiles = window.reshape(-1, TILE, in_dim)
    is_live = jnp.arange(SLOTS)[None, :] < tile_counts[:, None]
    gathered = window_tiles[tile_cols]
    gathered = jnp.where(is_live[:, :, None, None], gathered, jnp.zeros((), gathered.dtype))
    gathered = gathered.reshape(row_tiles, SLOTS * TILE, in_dim)
    values = tile_values.reshape(row_tiles, TILE, SLOTS * TILE)
    summed = jnp.einsum(
        "rik,rkf->rif", values, gathered, preferred_element_type=jnp.float32
    ).reshape(rows_dev, in_dim)
    aggregated = summed.astype(jnp.bfloat16)
    pre_act = jnp.dot(aggregated, weight, preferred_element_type=jnp.float32) + bias
    value_part, slope = gelu_parts(pre_act)
    activations = value_part.astype(jnp.bfloat16)
    pre_grad = (out_grad.astype(jnp.float32) * slope).astype(jnp.bfloat16)
    factor = 1.0 / math.sqrt(nodes)
    local_weight = (
        lax.dot_general(
            aggregated, pre_grad, (((0,), (0,)), ((), ())), preferred_element_type=jnp.float32
        )
        * factor
    )
    local_bias = jnp.sum(pre_grad.astype(jnp.float32), axis=0) * factor
    weight_grad, bias_grad = lax.psum((local_weight, local_bias), ("blk", "rep"))
    row_grad = lax.dot_general(
        pre_grad, weight, (((1,), (1,)), ((), ())), preferred_element_type=jnp.float32
    ).astype(jnp.bfloat16)
    grad_tiles = row_grad.reshape(row_tiles, TILE, in_dim)
    partial_value = jnp.einsum(
        "rik,rif->rkf", values, grad_tiles, preferred_element_type=jnp.float32
    )
    partial_value = partial_value.reshape(row_tiles, SLOTS, TILE, in_dim)
    partial_value = jnp.where(
        is_live[:, :, None, None], partial_value, jnp.zeros((), partial_value.dtype)
    )
    window_count = len(offsets) * block_rows // TILE
    placed = (
        jnp.zeros((window_count, TILE, in_dim), jnp.float32)
        .at[tile_cols.reshape(-1)]
        .add(partial_value.reshape(-1, TILE, in_dim))
    )
    terms = placed.reshape(len(offsets), block_rows, in_dim)
    block_total = terms[REACH]
    for position, offset_now in enumerate(offsets):
        if offset_now != 0:
            block_total = block_total + passed_along(
                terms[position].astype(jnp.bfloat16), "blk", offset_now
            ).astype(jnp.float32)
    feature_grad = summed_on_arrival(block_total, "rep", 0)
    return (activations, feature_grad, weight_grad, bias_grad)


def solution(mesh):
    in_specs = (
        P(("blk", "rep"), None),
        P(),
        P(),
        P(("blk", "rep"), None),
        P(("blk", "rep"), None),
        P(("blk", "rep")),
        P(("blk", "rep"), None),
    )
    out_specs = (P(("blk", "rep"), None), P(("blk", "rep"), None), P(), P())
    return jax.shard_map(
        on_device, mesh=mesh, in_specs=in_specs, out_specs=out_specs, check_vma=False
    )
```

profile of v0, /device:TPU:2, one launch (start us, length us, event | category | flops | bytes accessed | tf_op | source)
XLA Modules:
  0.0 501.1 jit_solution(1405045156096830641)
XLA Ops:
  7.2 0.0 copy-start
  7.2 0.0 all-gather.2.cloned.1.call-start
  7.2 1.6 collective-permute-start
  8.8 0.8 collective-permute-start.1
  9.6 5.9 %collective-permute-done = bf16[1024,128]{1,0:T(8,128)(2,1)S(1)} collective-permute-done((bf16[1024,128]{1,0:T(8,128)(2,1)}, bf16[1024,128]{1,0:T(8,128)(2,1)S(1)}, u32[]{:S(2)}, u32[]{:S(2)}) %collective-permute-start) | collective-permute-done | bytes 262176 | tf_op jit(solution)/shard_map/ppermute | solution.py:15
  15.6 1.2 collective-permute-done.1
  16.8 1.9 pad_maximum_fusion
  18.7 0.0 all-gather.2.cloned.1.call-update
  18.7 0.7 iota_compare_fusion
  19.4 0.1 copy.15
  19.5 0.1 lt.47
  19.6 0.8 reshape.95
  20.4 0.7 compare_select_fusion
  21.1 0.1 reshape.101
  21.2 0.1 broadcast_bitcast_fusion
  21.3 37.8 %all-gather.2.cloned.1.call-done = bf16[3,4096,128]{2,1,0:T(8,128)(2,1)} async-done(((bf16[3,1024,128]{2,1,0:T(8,128)(2,1)}), bf16[3,4096,128]{2,1,0:T(8,128)(2,1)}) %all-gather.2.cloned.1.call-update) | async-done | bytes 3145744 | tf_op jit(solution)/shard_map/all_gather | solution.py:53
  59.0 10.5 %gather_fusion = bf16[256,128,128]{2,1,0:T(8,128)(2,1)} fusion(bf16[96,128,128]{2,1,0:T(8,128)(2,1)} %bitcast.41, s32[1024]{0:T(1024)S(1)} %pad_clamp_fusion), kind=kCustom, calls=%fused_computation | custom fusion | bytes 16778240 | tf_op jit(solution)/shard_map/gather | solution.py:56
  69.6 16.3 %bitcast_select_fusion = bf16[8,4096,128]{2,1,0:T(8,128)(2,1)S(1)} fusion(pred[8,4096]{1,0:T(8,128)(4,1)S(1)} %broadcast_bitcast_fusion, bf16[8,4096,128]{2,1,0:T(8,128)(2,1)} %bitcast.40), kind=kLoop, calls=%fused_computation.3 | loop fusion | flops 4194304 | bytes 16809984 | tf_op jit(solution)/shard_map/jit(_where)/select_n | solution.py:57
  85.9 0.0 copy-start.2
  85.9 0.0 copy-start.3
  85.9 5.8 %convolution_convert_fusion = bf16[8,128,128]{1,2,0:T(8,128)(2,1)S(1)} fusion(bf16[8,128,4096]{2,1,0:T(8,128)(2,1)} %bitcast.36, bf16[8,4096,128]{2,1,0:T(8,128)(2,1)S(1)} %bitcast_select_fusion), kind=kOutput, calls=%fused_computation.18 | convolution fusion | flops 1073872896 | bytes 17039360 | tf_op jit(solution)/shard_map/rik,rkf->rif/dot_general | solution.py:60
  91.7 0.0 slice-start
  91.7 0.0 slice-start.1
  91.8 2.7 convert_reduce_fusion
  94.5 0.4 convolution_convert_fusion.1
  94.9 0.6 slice-done.1
  95.6 8.1 %convolution_bitcast_fusion = f32[8,4096,128]{1,2,0:T(8,128)} fusion(bf16[8,128,128]{2,1,0:T(8,128)(2,1)S(1)} %bitcast.42, bf16[8,128,4096]{2,1,0:T(8,128)(2,1)S(1)} %bitcast.39), kind=kOutput, calls=%fused_computation.2 | convolution fusion | flops 1073741824 | bytes 25427968 | tf_op jit(solution)/shard_map/rik,rif->rkf/dot_general | solution.py:81
  103.7 17.4 %copy.17 = f32[8,4096,128]{2,1,0:T(8,128)} copy(f32[8,4096,128]{1,2,0:T(8,128)} %convolution_bitcast_fusion) | data formatting | bytes 33554432 | tf_op jit(solution)/shard_map/rik,rif->rkf/dot_general | solution.py:81
  121.0 11.6 %broadcast_select_fusion = f32[256,128,128]{2,1,0:T(8,128)} fusion(f32[256,128,128]{2,1,0:T(8,128)} %bitcast.35, pred[256]{0:T(512)(128)(4,1)S(1)} %lt.47), kind=kLoop, calls=%fused_computation.4 | loop fusion | flops 4194304 | bytes 33554688 | tf_op jit(solution)/shard_map/jit(_where)/select_n | solution.py:85
  132.7 3.4 broadcast_in_dim.45
  136.1 52.3 %scatter_fusion = f32[96,128,128]{2,1,0:T(8,128)} fusion(f32[96,128,128]{2,1,0:T(8,128)} %broadcast_in_dim.45, s32[256]{0:T(256)S(1)} %bitcast.50, f32[256,128,128]{2,1,0:T(8,128)} %broadcast_select_fusion), kind=kCustom, calls=%fused_computation.1 | custom fusion | flops 4194304 | bytes 50332672 | tf_op jit(solution)/shard_map/scatter-add | solution.py:92
  188.4 3.5 convert.4
  191.9 0.2 fusion.9
  192.1 0.5 collective-permute-start.2
  192.6 1.6 collective-permute-start.3
  194.2 1.7 slice.19
  195.9 21.5 %collective-permute-done.2 = bf16[4096,128]{1,0:T(8,128)(2,1)S(1)} collective-permute-done((bf16[4096,128]{1,0:T(8,128)(2,1)S(1)}, bf16[4096,128]{1,0:T(8,128)(2,1)S(1)}, u32[]{:S(2)}, u32[]{:S(2)}) %collective-permute-start.2) | collective-permute-done | bytes 1048608 | tf_op jit(solution)/shard_map/ppermute | solution.py:15
  217.4 3.9 collective-permute-done.3
  221.3 1.6 fusion.7
  222.9 3.6 all-to-all-start
  226.5 0.0 copy-start.1
  226.5 0.0 all-reduce.2.cloned.1.call-start
  226.6 1.0 convolution_multiply_fusion
  227.6 0.0 all-reduce.2.cloned.1.call-update
  227.6 96.5 %psum.15 = f32[512]{0:T(512)} all-reduce(f32[512]{0:T(512)S(1)} %broadcast_multiply_fusion), channel_id=1, replica_groups=mesh['blk'=64,'rep'=4] {'blk','rep'}, use_global_device_ids=true, to_apply=%region_4.5 | all-reduce | flops 512 | bytes 4096 | tf_op jit(solution)/shard_map/psum | solution.py:76
  324.1 0.9 reduce_sum.18
  325.1 167.6 %all-reduce.2.cloned.1.call-done = f32[128,512]{1,0:T(8,128)} async-done(((f32[128,512]{1,0:T(8,128)}), f32[128,512]{1,0:T(8,128)}) %all-reduce.2.cloned.1.call-update) | async-done | bytes 262160 | tf_op jit(solution)/shard_map/psum | solution.py:76
  492.6 1.7 copy.21
  (10 shorter events, 0.0 us)
Async XLA Ops:
  7.2 84.6 %copy-start = (bf16[128,512]{1,0:T(8,128)(2,1)S(1)}, bf16[128,512]{1,0:T(8,128)(2,1)}, u32[]{:S(2)}) copy-start(bf16[128,512]{1,0:T(8,128)(2,1)} %param.8) | copy-start | bytes 393220
  7.2 51.9 %all-gather.2.cloned.1.call-start = ((), (), s32[]{:S(2)}) async-start(), calls=%async_computation.1 | async-start | bytes 3932160 | tf_op jit(solution)/shard_map/all_gather | solution.py:53
  7.2 8.3 %collective-permute-start = (bf16[1024,128]{1,0:T(8,128)(2,1)}, bf16[1024,128]{1,0:T(8,128)(2,1)S(1)}, u32[]{:S(2)}, u32[]{:S(2)}) collective-permute-start(bf16[1024,128]{1,0:T(8,128)(2,1)} %param.7), channel_id=1, source_target_pairs={{0,4},{4,8},{8,12},{12,16},{16,20},{20,24},{24,28},{28,32},{32,36}... | collective-permute-start | bytes 786440 | tf_op jit(solution)/shard_map/ppermute | solution.py:15
  8.8 8.0 %collective-permute-start.1 = (bf16[1024,128]{1,0:T(8,128)(2,1)}, bf16[1024,128]{1,0:T(8,128)(2,1)S(1)}, u32[]{:S(2)}, u32[]{:S(2)}) collective-permute-start(bf16[1024,128]{1,0:T(8,128)(2,1)} %param.7), channel_id=1, source_target_pairs={{0,252},{4,0},{8,4},{12,8},{16,12},{20,16},{24,20},{28,24},{32,28}... | collective-permute-start | bytes 786440 | tf_op jit(solution)/shard_map/ppermute | solution.py:15
  85.9 5.9 %copy-start.2 = (bf16[1024,512]{1,0:T(8,128)(2,1)S(1)}, bf16[1024,512]{1,0:T(8,128)(2,1)}, u32[]{:S(2)}) copy-start(bf16[1024,512]{1,0:T(8,128)(2,1)} %param.13) | copy-start | bytes 3145732
  85.9 5.9 %copy-start.3 = (f32[512]{0:T(512)S(1)}, f32[512]{0:T(512)}, u32[]{:S(2)}) copy-start(f32[512]{0:T(512)} %param.9) | copy-start | bytes 6148
  91.7 3.2 slice-start
  91.7 3.8 slice-start.1
  192.1 25.3 %collective-permute-start.2 = (bf16[4096,128]{1,0:T(8,128)(2,1)S(1)}, bf16[4096,128]{1,0:T(8,128)(2,1)S(1)}, u32[]{:S(2)}, u32[]{:S(2)}) collective-permute-start(bf16[4096,128]{1,0:T(8,128)(2,1)S(1)} %bitcast.46), channel_id=1, source_target_pairs={{0,252},{4,0},{8,4},{12,8},{16,12},{20,16},{24,20},{28,24},{32,28}... | collective-permute-start | bytes 3145736 | tf_op jit(solution)/shard_map/ppermute | solution.py:15
  192.6 28.7 %collective-permute-start.3 = (bf16[4096,128]{1,0:T(8,128)(2,1)S(1)}, bf16[4096,128]{1,0:T(8,128)(2,1)S(1)}, u32[]{:S(2)}, u32[]{:S(2)}) collective-permute-start(bf16[4096,128]{1,0:T(8,128)(2,1)S(1)} %bitcast.45), channel_id=1, source_target_pairs={{0,4},{4,8},{8,12},{12,16},{16,20},{20,24},{24,28},{28,32},{32,36}... | collective-permute-start | bytes 3145736 | tf_op jit(solution)/shard_map/ppermute | solution.py:15
  222.9 101.3 %all-to-all-start = ((f32[4,1024,128]{2,1,0:T(8,128)}), f32[4,1024,128]{2,1,0:T(8,128)S(1)}, u32[]{:S(2)}, u32[]{:S(2)}) async-start(f32[4,1024,128]{2,1,0:T(8,128)} %bitcast.16), calls=%async_computation | async-start | bytes 4194304 | tf_op jit(solution)/shard_map/all_to_all | solution.py:25
  226.5 267.8 %copy-start.1 = (bf16[128,512]{1,0:T(8,128)(2,1)S(1)}, bf16[128,512]{1,0:T(8,128)(2,1)}, u32[]{:S(2)}) copy-start(bf16[128,512]{1,0:T(8,128)(2,1)} %param.8) | copy-start | bytes 393220
  226.5 266.1 %all-reduce.2.cloned.1.call-start = ((), (), s32[]{:S(2)}) async-start(), calls=%async_computation.2 | async-start | bytes 524288 | tf_op jit(solution)/shard_map/psum | solution.py:76
Sparse Core Ops, SparseCore 0:
  18.8 40.1 all-gather.1
  233.3 259.2 all-reduce.1
where the time goes:
time: 502 us; the launch traced here: 501 us
  waiting for transfers between devices  238 us (47%)
  blocking collectives  96.5 us (19%)
  other arithmetic  89.6 us (18%)
  local copies, waits for them, and re-layouts  36.7 us (7%)
  matrix products  18.1 us (4%)
  between operations  14.2 us (3%)
  starting transfers between devices  8.2 us (2%)
    psum x1, waiting for transfers between devices, on_device(): lax.psum((local_weight, local_bias), ('blk', 'rep'))  168 us
    psum x1, blocking collectives, on_device(): lax.psum((local_weight, local_bias), ('blk', 'rep'))  96.5 us
    scatter-add x1, other arithmetic, on_device(): placed = jnp.zeros((window_count, TILE, in_dim), jnp.float32).at[tile_col...  52.3 us
    all_gather x1, waiting for transfers between devices, on_device(): lax.all_gather(stacked, 'rep', axis=1, tiled=True).reshape(-1, in_dim)  37.8 us
    ppermute x4, waiting for transfers between devices, passed_along(): return lax.ppermute(value, axis, pairs)  32.5 us
    dot_general x1, local copies, waits for them, and re-layouts, on_device(): jnp.einsum('rik,rif->rkf', values, grad_tiles, preferred_element_type=jnp...  17.4 us
    select_n x1, other arithmetic, on_device(): jnp.where(is_live[:, :, None, None], gathered, jnp.zeros((), gathered.dty...  16.3 us
    select_n x1, other arithmetic, on_device(): jnp.where(is_live[:, :, None, None], partial_value, jnp.zeros((), partial...  11.6 us
  transfers between devices with their start and end apart: 7, of which 6 were waited for; matrix products, arithmetic and copies ran while one was open for 1% of the time, Pallas kernels for 0%

commit v1 on v0

--- a/solution.py
+++ b/solution.py
@@ -73,7 +73,7 @@
         * factor
     )
     local_bias = jnp.sum(pre_grad.astype(jnp.float32), axis=0) * factor
-    weight_grad, bias_grad = lax.psum((local_weight, local_bias), ("blk", "rep"))
+    weight_grad, bias_grad = lax.psum(lax.psum((local_weight, local_bias), "blk"), "rep")
     row_grad = lax.dot_general(
         pre_grad, weight, (((1,), (1,)), ((), ())), preferred_element_type=jnp.float32
     ).astype(jnp.bfloat16)

time: 502 us -> 965 us (1.92)
  waiting for transfers between devices: 238 us -> 632 us
  blocking collectives: 96.5 us -> 161 us
    psum x1 -> x2, waiting for transfers between devices: 168 us -> 561 us  [the longest x1 561 us: on_device(): lax.psum((local_weight, local_bias), 'blk')]
    psum x1 -> x2, blocking collectives: 96.5 us -> 161 us  [the longest x1 153 us: on_device(): lax.psum((local_weight, local_bias), 'blk')]
  transfers between devices with their start and end apart: 7 -> 8, of which waited for: 6 -> 6; matrix products, arithmetic and copies ran while one was open for 1% -> 1% of each run, Pallas kernels for 0% -> 0%
where the time goes in v1:
time: 965 us; the launch traced here: 959 us
  waiting for transfers between devices  632 us (65%)
  blocking collectives  161 us (17%)
  other arithmetic  89.7 us (9%)
  local copies, waits for them, and re-layouts  36.7 us (4%)
  matrix products  18.1 us (2%)
  between operations  13.9 us (1%)
    psum x1, waiting for transfers between devices, on_device(): lax.psum((local_weight, local_bias), 'blk')  561 us
    psum x1, blocking collectives, on_device(): lax.psum((local_weight, local_bias), 'blk')  153 us
    scatter-add x1, other arithmetic, on_device(): placed = jnp.zeros((window_count, TILE, in_dim), jnp.float32).at[tile_col...  52.5 us
    all_gather x1, waiting for transfers between devices, on_device(): lax.all_gather(stacked, 'rep', axis=1, tiled=True).reshape(-1, in_dim)  37.8 us
    ppermute x4, waiting for transfers between devices, passed_along(): return lax.ppermute(value, axis, pairs)  32.6 us
  transfers between devices with their start and end apart: 8, of which 6 were waited for; matrix products, arithmetic and copies ran while one was open for 1% of the time, Pallas kernels for 0%

profile of v1, /device:TPU:2, one launch (start us, length us, event | category | flops | bytes accessed | tf_op | source)
XLA Modules:
  0.0 959.4 jit_solution(11307551306831335850)
XLA Ops:
  7.2 0.0 copy-start
  7.2 0.0 all-gather.2.cloned.1.call-start
  7.2 1.6 collective-permute-start
  8.8 0.8 collective-permute-start.1
  9.6 5.9 collective-permute-done
  15.6 1.2 collective-permute-done.1
  16.8 1.9 pad_maximum_fusion
  18.7 0.0 all-gather.2.cloned.1.call-update
  18.7 0.7 iota_compare_fusion
  19.4 0.1 copy.15
  19.5 0.1 lt.47
  19.6 0.8 reshape.95
  20.4 0.7 compare_select_fusion
  21.1 0.1 reshape.101
  21.2 0.1 broadcast_bitcast_fusion
  21.3 37.8 %all-gather.2.cloned.1.call-done = bf16[3,4096,128]{2,1,0:T(8,128)(2,1)} async-done(((bf16[3,1024,128]{2,1,0:T(8,128)(2,1)}), bf16[3,4096,128]{2,1,0:T(8,128)(2,1)}) %all-gather.2.cloned.1.call-update) | async-done | bytes 3145744 | tf_op jit(solution)/shard_map/all_gather | solution.py:53
  59.0 10.5 %gather_fusion = bf16[256,128,128]{2,1,0:T(8,128)(2,1)} fusion(bf16[96,128,128]{2,1,0:T(8,128)(2,1)} %bitcast.41, s32[1024]{0:T(1024)S(1)} %pad_clamp_fusion), kind=kCustom, calls=%fused_computation | custom fusion | bytes 16778240 | tf_op jit(solution)/shard_map/gather | solution.py:56
  69.5 16.3 %bitcast_select_fusion = bf16[8,4096,128]{2,1,0:T(8,128)(2,1)S(1)} fusion(pred[8,4096]{1,0:T(8,128)(4,1)S(1)} %broadcast_bitcast_fusion, bf16[8,4096,128]{2,1,0:T(8,128)(2,1)} %bitcast.40), kind=kLoop, calls=%fused_computation.3 | loop fusion | flops 4194304 | bytes 16809984 | tf_op jit(solution)/shard_map/jit(_where)/select_n | solution.py:57
  85.9 5.8 convolution_convert_fusion
  91.7 0.0 slice-start
  91.7 2.7 convert_reduce_fusion
  94.5 0.4 convolution_convert_fusion.1
  94.9 0.6 slice-done.1
  95.5 8.1 convolution_bitcast_fusion
  103.6 17.4 %copy.17 = f32[8,4096,128]{2,1,0:T(8,128)} copy(f32[8,4096,128]{1,2,0:T(8,128)} %convolution_bitcast_fusion) | data formatting | bytes 33554432 | tf_op jit(solution)/shard_map/rik,rif->rkf/dot_general | solution.py:81
  121.0 11.6 %broadcast_select_fusion = f32[256,128,128]{2,1,0:T(8,128)} fusion(f32[256,128,128]{2,1,0:T(8,128)} %bitcast.35, pred[256]{0:T(512)(128)(4,1)S(1)} %lt.47), kind=kLoop, calls=%fused_computation.4 | loop fusion | flops 4194304 | bytes 33554688 | tf_op jit(solution)/shard_map/jit(_where)/select_n | solution.py:85
  132.6 3.4 broadcast_in_dim.45
  136.1 52.5 %scatter_fusion = f32[96,128,128]{2,1,0:T(8,128)} fusion(f32[96,128,128]{2,1,0:T(8,128)} %broadcast_in_dim.45, s32[256]{0:T(256)S(1)} %bitcast.50, f32[256,128,128]{2,1,0:T(8,128)} %broadcast_select_fusion), kind=kCustom, calls=%fused_computation.1 | custom fusion | flops 4194304 | bytes 50332672 | tf_op jit(solution)/shard_map/scatter-add | solution.py:92
  188.5 3.5 convert.4
  192.0 0.2 fusion.9
  192.2 0.5 collective-permute-start.2
  192.7 1.6 collective-permute-start.3
  194.3 1.7 slice.19
  196.0 21.4 %collective-permute-done.2 = bf16[4096,128]{1,0:T(8,128)(2,1)S(1)} collective-permute-done((bf16[4096,128]{1,0:T(8,128)(2,1)S(1)}, bf16[4096,128]{1,0:T(8,128)(2,1)S(1)}, u32[]{:S(2)}, u32[]{:S(2)}) %collective-permute-start.2) | collective-permute-done | bytes 1048608 | tf_op jit(solution)/shard_map/ppermute | solution.py:15
  217.5 4.0 collective-permute-done.3
  221.5 1.6 fusion.7
  223.1 3.6 all-to-all-start
  226.7 0.0 copy-start.1
  226.7 0.0 all-reduce.3.cloned.1.call-start
  226.8 1.0 convolution_multiply_fusion
  227.8 0.0 all-reduce.3.cloned.1.call-update
  227.8 0.0 all-reduce.5.cloned.1.call-start
  227.9 561.4 %all-reduce.3.cloned.1.call-done = f32[128,512]{1,0:T(8,128)} async-done(((f32[128,512]{1,0:T(8,128)}), f32[128,512]{1,0:T(8,128)}) %all-reduce.3.cloned.1.call-update) | async-done | bytes 262160 | tf_op jit(solution)/shard_map/psum | solution.py:76
  789.3 0.0 all-reduce.5.cloned.1.call-update
  789.3 153.3 %psum.30 = f32[512]{0:T(512)S(1)} all-reduce(f32[512]{0:T(512)S(1)} %broadcast_multiply_fusion), channel_id=1, replica_groups=mesh['blk'=64,'rep'=4] {'blk'}, use_global_device_ids=true, to_apply=%region_5.6 | all-reduce | flops 512 | bytes 4096 | tf_op jit(solution)/shard_map/psum | solution.py:76
  942.6 7.7 psum.31
  950.3 0.9 reduce_sum.18
  951.2 1.7 copy.22
  (14 shorter events, 0.0 us)
Async XLA Ops:
  7.2 84.5 %copy-start = (bf16[128,512]{1,0:T(8,128)(2,1)S(1)}, bf16[128,512]{1,0:T(8,128)(2,1)}, u32[]{:S(2)}) copy-start(bf16[128,512]{1,0:T(8,128)(2,1)} %param.8) | copy-start | bytes 393220
  7.2 51.9 %all-gather.2.cloned.1.call-start = ((), (), s32[]{:S(2)}) async-start(), calls=%async_computation.1 | async-start | bytes 3932160 | tf_op jit(solution)/shard_map/all_gather | solution.py:53
  7.2 8.3 collective-permute-start
  8.8 8.0 collective-permute-start.1
  85.8 5.9 copy-start.2
  85.9 5.9 copy-start.3
  91.7 3.2 slice-start
  91.7 3.8 slice-start.1
  192.2 25.3 %collective-permute-start.2 = (bf16[4096,128]{1,0:T(8,128)(2,1)S(1)}, bf16[4096,128]{1,0:T(8,128)(2,1)S(1)}, u32[]{:S(2)}, u32[]{:S(2)}) collective-permute-start(bf16[4096,128]{1,0:T(8,128)(2,1)S(1)} %bitcast.46), channel_id=1, source_target_pairs={{0,252},{4,0},{8,4},{12,8},{16,12},{20,16},{24,20},{28,24},{32,28}... | collective-permute-start | bytes 3145736 | tf_op jit(solution)/shard_map/ppermute | solution.py:15
  192.7 28.7 %collective-permute-start.3 = (bf16[4096,128]{1,0:T(8,128)(2,1)S(1)}, bf16[4096,128]{1,0:T(8,128)(2,1)S(1)}, u32[]{:S(2)}, u32[]{:S(2)}) collective-permute-start(bf16[4096,128]{1,0:T(8,128)(2,1)S(1)} %bitcast.45), channel_id=1, source_target_pairs={{0,4},{4,8},{8,12},{12,16},{16,20},{20,24},{24,28},{28,32},{32,36}... | collective-permute-start | bytes 3145736 | tf_op jit(solution)/shard_map/ppermute | solution.py:15
  223.1 727.2 %all-to-all-start = ((f32[4,1024,128]{2,1,0:T(8,128)}), f32[4,1024,128]{2,1,0:T(8,128)S(1)}, u32[]{:S(2)}, u32[]{:S(2)}) async-start(f32[4,1024,128]{2,1,0:T(8,128)} %bitcast.16), calls=%async_computation | async-start | bytes 4194304 | tf_op jit(solution)/shard_map/all_to_all | solution.py:25
  226.7 726.2 %copy-start.1 = (bf16[128,512]{1,0:T(8,128)(2,1)S(1)}, bf16[128,512]{1,0:T(8,128)(2,1)}, u32[]{:S(2)}) copy-start(bf16[128,512]{1,0:T(8,128)(2,1)} %param.8) | copy-start | bytes 393220
  226.7 562.6 %all-reduce.3.cloned.1.call-start = ((), (), s32[]{:S(2)}) async-start(), calls=%async_computation.2 | async-start | bytes 524288 | tf_op jit(solution)/shard_map/psum | solution.py:76
  227.8 723.4 %all-reduce.5.cloned.1.call-start = ((), (), s32[]{:S(2)}) async-start(), calls=%async_computation.3 | async-start | bytes 524288 | tf_op jit(solution)/shard_map/psum | solution.py:76
Sparse Core Ops, SparseCore 0:
  18.8 40.1 all-gather.1
  230.7 558.5 all-reduce.2
  791.9 44.4 all-reduce.4
